TPU v7x, 256 devices: a whole 4x4x8 slice. The times are simulated.
256 devices in a mesh: row: 8 (over z), col: 32 (over x, y, core).
Axes of the slice: x: 4, y: 4, z: 8, core: 2. Of those that a mesh axis runs over, the one named last changes fastest.
Arguments:
- h_values: float32 [8, 512, 4096], P('row', 'col'), as said below
- h_places: int32 [8, 512], P('row', 'col'), may hold values from 0 to 15, as said below
- h_counts: int32 [8, 32], P('row', 'col'), may hold values from 0 to 16, as said below
- p_values: float32 [8, 512, 4096], P('row', 'col'), as said below
- p_places: int32 [8, 512], P('row', 'col'), may hold values from 0 to 15, as said below
- p_counts: int32 [8, 32], P('row', 'col'), may hold values from 0 to 16, as said below
- s_values: float32 [8, 512, 4096], P('row', 'col'), as said below
- s_places: int32 [8, 512], P('row', 'col'), may hold values from 0 to 15, as said below
- s_counts: int32 [8, 32], P('row', 'col'), may hold values from 0 to 16, as said below
- x_places: int32 [8, 512], P('row', 'col'), may hold values from 0 to 15, as said below
- x_counts: int32 [8, 32], P('row', 'col'), may hold values from 0 to 16, as said below
Outputs:
- gradient: float32 [8, 512, 4096], P('row', 'col')
Inputs may be any that keep to these rules, and one draw needn't show every extreme that they name: `h_places`: in each tile the 16 entries are a permutation of the tile's positions; the first count entries are the present blocks. Every pattern is symmetric, holds every block whose block row and block column lie in the same row panel, and every block (i, j) whose cyclic block distance min(|i - j|, 64 - |i - j|) is 2 or less or exactly 32. `p_places`: as for h_places. `s_places`: as for h_places. `x_places`: as for h_places. `h_counts`: every tile whose block columns lie in its own row panel is full. `p_counts`: as for h_counts. `s_counts`: as for h_counts. `x_counts`: as for h_counts. `h_values`: the assembled H is symmetric. `p_values`: the assembled P is symmetric. `s_values`: the assembled S is symmetric.
All inputs are finite; a program needn't handle non-finite values.
Results may differ from a plain program's by a relative error of at most 0.000088.
Values sent between devices are 32-bit elements; how exact they have to be, the bound alone decides.
A program may use at most 64 MiB of HBM per device.

v0:
```python
import jax
import jax.numpy as jnp
from jax import lax
from jax.sharding import PartitionSpec as P

BS = 64
TC = 2


def from_root(value, axis, source):
    kept = jnp.where(lax.axis_index(axis) == source, value, 0).astype(value.dtype)
    return lax.psum(kept, axis)


def assemble(values, places, counts):
    blocks_in = values[0]
    capacity = blocks_in.shape[0]
    slot_ids = lax.iota(jnp.int32, capacity)
    matches = (places[0][:, None] == slot_ids[None, :]) & (slot_ids[:, None] < counts[0, 0])
    spread = jnp.dot(matches.astype(jnp.float32).T, blocks_in, precision=lax.Precision.HIGHEST)
    row_count = capacity // TC
    return (
        spread.reshape(row_count, TC, BS, BS).transpose(0, 2, 1, 3).reshape(row_count * BS, TC * BS)
    )


def expand_mask(present, row_count, col_count):
    flags = present.reshape(row_count, col_count)
    return jnp.broadcast_to(flags[:, None, :, None], (row_count, BS, col_count, BS)).reshape(
        row_count * BS, col_count * BS
    )


def tile_mask(places, counts):
    capacity = places.shape[1]
    slot_ids = lax.iota(jnp.int32, capacity)
    matches = (places[0][:, None] == slot_ids[None, :]) & (slot_ids[:, None] < counts[0, 0])
    present = jnp.sum(matches.astype(jnp.float32), axis=0)
    return expand_mask(present, capacity // TC, TC)


def tile_to_slots(tile, places, counts):
    row_count = tile.shape[0] // BS
    blocks = (
        tile.reshape(row_count, BS, TC, BS).transpose(0, 2, 1, 3).reshape(row_count * TC, BS * BS)
    )
    picked = jnp.take(blocks, places[0], axis=0)
    slot_ids = lax.iota(jnp.int32, places.shape[1])
    used = (slot_ids < counts[0, 0]).astype(jnp.float32)
    return (picked * used[:, None])[None]


def shards(
    h_values,
    h_places,
    h_counts,
    p_values,
    p_places,
    p_counts,
    s_values,
    s_places,
    s_counts,
    x_places,
    x_counts,
):
    col_index = lax.axis_index("col")
    h_tile = assemble(h_values, h_places, h_counts)
    p_tile = assemble(p_values, p_places, p_counts)
    s_tile = assemble(s_values, s_places, s_counts)
    mask_tile = tile_mask(x_places, x_counts)
    row_width = h_tile.shape[0]
    col_width = h_tile.shape[1]
    p_columns, s_columns = (
        lax.all_gather(p_tile, "row", axis=0, tiled=True),
        lax.all_gather(s_tile, "row", axis=0, tiled=True),
    )
    product = jnp.dot(
        lax.all_gather(h_tile, "col", axis=1, tiled=True),
        p_columns,
        precision=lax.Precision.HIGHEST,
    )
    y_tile = mask_tile * product
    y_panel = lax.all_gather(y_tile, "col", axis=1, tiled=True)
    x_tile = mask_tile * jnp.dot(y_panel, s_columns, precision=lax.Precision.HIGHEST)
    per_panel = row_width // col_width
    source_row = col_index // per_panel
    offset = col_index % per_panel * col_width
    y_part = lax.dynamic_slice_in_dim(y_panel, offset, col_width, 0)
    y_mirror = from_root(y_part, "row", source_row)
    far_part = lax.dot_general(
        lax.all_gather(s_tile, "col", axis=1, tiled=True),
        y_mirror,
        (((1,), (1,)), ((), ())),
        precision=lax.Precision.HIGHEST,
    )
    mirrored = mask_tile * far_part
    return tile_to_slots(x_tile + mirrored, x_places, x_counts)


def solution(mesh):
    in_specs = (
        P("row", "col", None),
        P("row", "col"),
        P("row", "col"),
        P("row", "col", None),
        P("row", "col"),
        P("row", "col"),
        P("row", "col", None),
        P("row", "col"),
        P("row", "col"),
        P("row", "col"),
        P("row", "col"),
    )
    out_specs = P("row", "col", None)
    return jax.shard_map(shards, mesh=mesh, in_specs=in_specs, out_specs=out_specs, check_vma=False)
```

profile of v0, /device:TPU:2, one launch (start us, length us, event | category | flops | bytes accessed | tf_op | source)
XLA Modules:
  0.0 405.1 jit_solution(8840308818379448259)
XLA Ops:
  7.3 1.1 dot_general.34
  8.4 1.3 convolution_bitcast_fusion.1
  9.8 0.3 copy.26
  10.0 0.9 reshape.190
  11.6 0.2 dot_general.31
  11.9 0.7 convolution_bitcast_fusion.2
  12.6 0.3 copy.24
  12.8 0.9 reshape.189
  14.4 0.1 convert_reduce_fusion
  14.5 0.1 broadcast_in_dim.19
  14.6 0.2 broadcast_in_dim.20
  14.8 0.3 reshape.188
  15.2 40.0 %all-gather.8.cloned.1.call-done = f32[4096,128]{0,1:T(8,128)} async-done(((f32[512,128]{0,1:T(8,128)}), f32[4096,128]{0,1:T(8,128)}) %all-gather.8.cloned.1.call-update) | async-done | bytes 2097168 | tf_op jit(solution)/shard_map/all_gather | solution.py:74
  55.1 59.1 %all-gather.6.cloned.1.call-done = f32[512,4096]{0,1:T(8,128)} async-done(((f32[512,128]{0,1:T(8,128)}), f32[512,4096]{0,1:T(8,128)}) %all-gather.6.cloned.1.call-update) | async-done | bytes 8388624 | tf_op jit(solution)/shard_map/all_gather | solution.py:78
  114.2 16.5 %convolution_multiply_fusion = f32[512,128]{1,0:T(8,128)} fusion(f32[512,128]{1,0:T(8,128)S(1)} %reshape.188, f32[512,4096]{0,1:T(8,128)} %all-gather.6.cloned.1.call-done, f32[4096,128]{0,1:T(8,128)} %all-gather.8.cloned.1.call-done), kind=kOutput, calls=%fused_computation.7 | convolution fusion | flops 3221291008 | bytes 11010048 | tf_op jit(solution)/shard_map/dot_general | solution.py:77
  131.5 0.2 dot_general.38
  131.7 0.7 convolution_bitcast_fusion
  132.4 0.3 copy.28
  132.7 0.9 reshape.191
  133.6 0.5 all-gather.14.cloned.1.call-update
  134.2 0.2 all-reduce.2.cloned.1.call-start
  134.4 60.4 %all-gather.10.cloned.1.call-done = f32[512,4096]{1,0:T(8,128)} async-done(((f32[512,128]{1,0:T(8,128)}), f32[512,4096]{1,0:T(8,128)}) %all-gather.10.cloned.1.call-update) | async-done | bytes 8388624 | tf_op jit(solution)/shard_map/all_gather | solution.py:83
  194.8 3.2 dynamic-slice_select_fusion
  198.0 39.7 %all-gather.12.cloned.1.call-done = f32[4096,128]{0,1:T(8,128)} async-done(((f32[512,128]{0,1:T(8,128)}), f32[4096,128]{0,1:T(8,128)}) %all-gather.12.cloned.1.call-update) | async-done | bytes 2097168 | tf_op jit(solution)/shard_map/all_gather | solution.py:75
  237.7 9.3 %fusion.29 = f32[512,128]{1,0:T(8,128)S(1)} fusion(f32[512,4096]{1,0:T(8,128)} %all-gather.10.cloned.1.call-done, f32[4096,128]{0,1:T(8,128)} %all-gather.12.cloned.1.call-done), kind=kOutput, calls=%fused_computation.48 | convolution fusion | flops 3221225472 | bytes 10747904 | tf_op jit(solution)/shard_map/dot_general | solution.py:84
  247.0 49.5 %all-gather.14.cloned.1.call-done = f32[512,4096]{0,1:T(8,128)} async-done(((f32[512,128]{0,1:T(8,128)}), f32[512,4096]{0,1:T(8,128)}) %all-gather.14.cloned.1.call-update) | async-done | bytes 8388624 | tf_op jit(solution)/shard_map/all_gather | solution.py:91
  296.6 83.7 %all-reduce.2.cloned.1.call-done = f32[128,4096]{1,0:T(8,128)} async-done(((f32[128,4096]{1,0:T(8,128)}), f32[128,4096]{1,0:T(8,128)}) %all-reduce.2.cloned.1.call-update) | async-done | bytes 2097168 | tf_op jit(solution)/shard_map/psum | solution.py:12
  380.3 16.0 %fusion = f32[512,128]{1,0:T(8,128)S(1)} fusion(f32[512,128]{1,0:T(8,128)S(1)} %reshape.188, f32[512,128]{1,0:T(8,128)S(1)} %fusion.29, f32[512,4096]{0,1:T(8,128)} %all-gather.14.cloned.1.call-done, f32[128,4096]{1,0:T(8,128)} %all-reduce.2.cloned.1.call-done), kind=kOutput, calls=%fused_computation.6 | convolution fusion | flops 3221356544 | bytes 11272192 | tf_op jit(solution)/shard_map/dot_general | solution.py:90
  396.3 0.3 reshape.192
  396.7 0.2 reshape.193
  396.9 0.6 gather_fusion
  397.5 0.8 fusion.7
  (29 shorter events, 0.4 us)
Async XLA Ops:
  6.5 5.1 %copy-start = (f32[1,16,4096]{2,1,0:T(8,128)S(1)}, f32[1,16,4096]{2,1,0:T(8,128)}, u32[]{:S(2)}) copy-start(f32[1,16,4096]{2,1,0:T(8,128)} %param.11) | copy-start | bytes 786436
  6.5 48.6 %all-gather.8.cloned.1.call-start = ((), (), s32[]{:S(2)}) async-start(), calls=%async_computation.1 | async-start | bytes 2359296 | tf_op jit(solution)/shard_map/all_gather | solution.py:74
  8.4 3.5 copy-start.2
  10.9 3.5 copy-start.4
  10.9 103.3 %all-gather.6.cloned.1.call-start = ((), (), s32[]{:S(2)}) async-start(), calls=%async_computation | async-start | bytes 8650752 | tf_op jit(solution)/shard_map/all_gather | solution.py:78
  13.7 181.1 %all-gather.10.cloned.1.call-start = ((), (), s32[]{:S(2)}) async-start(), calls=%async_computation.2 | async-start | bytes 8650752 | tf_op jit(solution)/shard_map/all_gather | solution.py:83
  15.1 116.3 %copy-start.1 = (f32[1,16,4096]{2,1,0:T(8,128)S(1)}, f32[1,16,4096]{2,1,0:T(8,128)}, u32[]{:S(2)}) copy-start(f32[1,16,4096]{2,1,0:T(8,128)} %param.17) | copy-start | bytes 786436
  15.2 116.5 %copy-start.3 = (s32[1,16]{1,0:T(1,128)S(1)}, s32[1,16]{1,0:T(1,128)}, u32[]{:S(2)}) copy-start(s32[1,16]{1,0:T(1,128)} %param.18) | copy-start | bytes 196
  130.8 106.9 %all-gather.12.cloned.1.call-start = ((), (), s32[]{:S(2)}) async-start(), calls=%async_computation.3 | async-start | bytes 2359296 | tf_op jit(solution)/shard_map/all_gather | solution.py:75
  133.6 163.0 %all-gather.14.cloned.1.call-start = ((), (), s32[]{:S(2)}) async-start(), calls=%async_computation.4 | async-start | bytes 8650752 | tf_op jit(solution)/shard_map/all_gather | solution.py:91
  134.2 246.2 %all-reduce.2.cloned.1.call-start = ((), (), s32[]{:S(2)}) async-start(), calls=%async_computation.5 | async-start | bytes 4194304 | tf_op jit(solution)/shard_map/psum | solution.py:12
Sparse Core Ops, SparseCore 0:
  11.1 44.0 all-gather.7
  57.7 56.4 all-gather.5
  130.9 63.8 all-gather.9
  196.5 41.1 all-gather.11
  240.1 56.4 all-gather.13
  298.8 81.4 all-reduce.1
where the time goes:
time: 405 us
  waiting for transfers between devices  333 us (82%)
  matrix products  44.6 us (11%)
  between operations  16.4 us (4%)
  local copies, waits for them, and re-layouts  6.76 us (2%)
  other arithmetic  4.09 us (1%)
    psum x1, waiting for transfers between devices, from_root(): return lax.psum(kept, axis)  83.7 us
    all_gather x1, waiting for transfers between devices, shards(): y_panel = lax.all_gather(y_tile, 'col', axis=1, tiled=True)  60.4 us
    all_gather x1, waiting for transfers between devices, shards(): lax.all_gather(h_tile, 'col', axis=1, tiled=True)  59.1 us
    all_gather x1, waiting for transfers between devices, shards(): lax.all_gather(s_tile, 'col', axis=1, tiled=True)  49.5 us
    all_gather x1, waiting for transfers between devices, shards(): lax.all_gather(p_tile, 'row', axis=0, tiled=True)  40 us
    all_gather x1, waiting for transfers between devices, shards(): lax.all_gather(s_tile, 'row', axis=0, tiled=True)  39.7 us
    dot_general x1, matrix products, shards(): jnp.dot(lax.all_gather(h_tile, 'col', axis=1, tiled=True), p_columns, pre...  16.5 us
    dot_general x1, matrix products, shards(): lax.dot_general(lax.all_gather(s_tile, 'col', axis=1, tiled=True), y_mirr...  16 us
  transfers between devices with their start and end apart: 6, of which 6 were waited for; matrix products, arithmetic and copies ran while one was open for 4% of the time, Pallas kernels for 0%

commit v1 on v0

--- a/solution.py
+++ b/solution.py
@@ -80,7 +80,8 @@
         precision=lax.Precision.HIGHEST,
     )
     y_tile = mask_tile * product
-    y_panel = lax.all_gather(y_tile, "col", axis=1, tiled=True)
+    outgoing = jnp.stack([y_tile] * lax.axis_size("col"))
+    y_panel = jnp.concatenate(lax.all_to_all(outgoing, "col", 0, 0), axis=1)
     x_tile = mask_tile * jnp.dot(y_panel, s_columns, precision=lax.Precision.HIGHEST)
     per_panel = row_width // col_width
     source_row = col_index // per_panel

time: 405 us -> 397 us (0.980)
  waiting for transfers between devices: 333 us -> 309 us
  matrix products: 44.6 us -> 50.6 us
  starting transfers between devices: 0.39 us -> 6.01 us
  local copies, waits for them, and re-layouts: 6.76 us -> 11.2 us
    all_to_all x0 -> x1, waiting for transfers between devices: none -> 111 us  [shards(): y_panel = jnp.concatenate(lax.all_to_all(outgoing, 'col', 0, 0), axis=1)]
    all_gather x1 -> x0, waiting for transfers between devices: 60.4 us -> none  [shards(): y_panel = lax.all_gather(y_tile, 'col', axis=1, tiled=True)]
    all_gather x1, waiting for transfers between devices: 49.5 us -> 0.08 us  [shards(): lax.all_gather(s_tile, 'col', axis=1, tiled=True)]
    all_gather x1, waiting for transfers between devices: 39.7 us -> 0.02 us  [shards(): lax.all_gather(s_tile, 'row', axis=0, tiled=True)]
    psum x1, waiting for transfers between devices: 83.7 us -> 102 us  [from_root(): return lax.psum(kept, axis)]
    dot_general x1, matrix products: 9.35 us -> 16.1 us  [shards(): jnp.dot(y_panel, s_columns, precision=lax.Precision.HIGHEST)]
    all_to_all x0 -> x1, starting transfers between devices: none -> 5.84 us  [shards(): y_panel = jnp.concatenate(lax.all_to_all(outgoing, 'col', 0, 0), axis=1)]
    another operation x0 -> x1, local copies, waits for them, and re-layouts: none -> 4.3 us  [shards(): outgoing = jnp.stack([y_tile] * lax.axis_size('col'))]
  transfers between devices with their start and end apart: 6 -> 6, of which waited for: 6 -> 5; matrix products, arithmetic and copies ran while one was open for 4% -> 11% of each run, Pallas kernels for 0% -> 0%
where the time goes in v1:
time: 397 us
  waiting for transfers between devices  309 us (78%)
  matrix products  50.6 us (13%)
  between operations  16 us (4%)
  local copies, waits for them, and re-layouts  11.2 us (3%)
  starting transfers between devices  6.01 us (2%)
  other arithmetic  4.06 us (1%)
    all_to_all x1, waiting for transfers between devices, shards(): y_panel = jnp.concatenate(lax.all_to_all(outgoing, 'col', 0, 0), axis=1)  111 us
    psum x1, waiting for transfers between devices, from_root(): return lax.psum(kept, axis)  102 us
    all_gather x1, waiting for transfers between devices, shards(): lax.all_gather(h_tile, 'col', axis=1, tiled=True)  59.1 us
    all_gather x1, waiting for transfers between devices, shards(): lax.all_gather(p_tile, 'row', axis=0, tiled=True)  36.6 us
    dot_general x1, matrix products, shards(): jnp.dot(y_panel, s_columns, precision=lax.Precision.HIGHEST)  16.1 us
    dot_general x1, matrix products, shards(): lax.dot_general(lax.all_gather(s_tile, 'col', axis=1, tiled=True), y_mirr...  16 us
    dot_general x1, matrix products, shards(): jnp.dot(lax.all_gather(h_tile, 'col', axis=1, tiled=True), p_columns, pre...  15.8 us
  transfers between devices with their start and end apart: 6, of which 5 were waited for; matrix products, arithmetic and copies ran while one was open for 11% of the time, Pallas kernels for 0%

profile of v1, /device:TPU:2, one launch (start us, length us, event | category | flops | bytes accessed | tf_op | source)
XLA Modules:
  0.0 396.8 jit_solution(16011420224244355452)
XLA Ops:
  6.5 1.2 dot_general.34
  8.4 1.3 convolution_bitcast_fusion.1
  9.8 0.3 copy.27
  10.0 0.9 reshape.198
  11.0 0.2 dot_general.31
  11.9 0.7 convolution_bitcast_fusion.2
  12.6 0.3 copy.25
  12.9 0.9 reshape.197
  13.8 0.2 dot_general.38
  14.7 0.7 convolution_bitcast_fusion
  15.4 0.3 copy.30
  15.7 0.9 reshape.201
  16.6 0.5 all-gather.11.cloned.1.call-update
  17.8 0.1 convert_reduce_fusion
  17.9 0.1 broadcast_in_dim.19
  18.0 0.2 broadcast_in_dim.20
  18.2 0.3 reshape.196
  18.5 36.6 %all-gather.7.cloned.1.call-done = f32[4096,128]{0,1:T(8,128)} async-done(((f32[512,128]{0,1:T(8,128)}), f32[4096,128]{0,1:T(8,128)}) %all-gather.7.cloned.1.call-update) | async-done | bytes 2097168 | tf_op jit(solution)/shard_map/all_gather | solution.py:74
  55.1 59.1 %all-gather.5.cloned.1.call-done = f32[512,4096]{0,1:T(8,128)} async-done(((f32[512,128]{0,1:T(8,128)}), f32[512,4096]{0,1:T(8,128)}) %all-gather.5.cloned.1.call-update) | async-done | bytes 8388624 | tf_op jit(solution)/shard_map/all_gather | solution.py:78
  114.2 15.8 %convolution_multiply_fusion = f32[512,128]{1,0:T(8,128)S(1)} fusion(f32[512,128]{1,0:T(8,128)S(1)} %reshape.196, f32[512,4096]{0,1:T(8,128)} %all-gather.5.cloned.1.call-done, f32[4096,128]{0,1:T(8,128)} %all-gather.7.cloned.1.call-done), kind=kOutput, calls=%fused_computation.7 | convolution fusion | flops 3221291008 | bytes 11010048 | tf_op jit(solution)/shard_map/dot_general | solution.py:77
  130.0 0.1 copy.28
  130.2 4.3 %stack.2 = f32[32,512,128]{1,2,0:T(8,128)} broadcast(f32[512,128]{0,1:T(8,128)S(1)} %copy.28), dimensions={1,2} | broadcast | bytes 8650752 | tf_op jit(solution)/shard_map/stack | solution.py:83
  134.5 5.8 %all-to-all-start = ((f32[32,512,128]{1,2,0:T(8,128)}), f32[32,512,128]{1,2,0:T(8,128)}, u32[]{:S(2)}, u32[]{:S(2)}) async-start(f32[32,512,128]{1,2,0:T(8,128)} %stack.2), calls=%async_computation | async-start | bytes 16777216 | tf_op jit(solution)/shard_map/all_to_all | solution.py:84
  140.4 110.8 %all-to-all-done = f32[32,512,128]{1,2,0:T(8,128)} async-done(((f32[32,512,128]{1,2,0:T(8,128)}), f32[32,512,128]{1,2,0:T(8,128)}, u32[]{:S(2)}, u32[]{:S(2)}) %all-to-all-start) | async-done | bytes 8388640 | tf_op jit(solution)/shard_map/all_to_all | solution.py:84
  251.2 3.1 dynamic-slice_select_fusion
  254.4 16.1 %fusion.29 = f32[512,128]{1,0:T(8,128)S(1)} fusion(f32[512,4096]{0,1:T(8,128)} %bitcast.19, f32[4096,128]{0,1:T(8,128)} %all-gather.9.cloned.1.call-done), kind=kOutput, calls=%fused_computation.48 | convolution fusion | flops 3221225472 | bytes 10747904 | tf_op jit(solution)/shard_map/dot_general | solution.py:85
  270.5 101.8 %all-reduce.2.cloned.1.call-done = f32[128,4096]{0,1:T(8,128)} async-done(((f32[128,4096]{0,1:T(8,128)}), f32[128,4096]{0,1:T(8,128)}) %all-reduce.2.cloned.1.call-update) | async-done | bytes 2097168 | tf_op jit(solution)/shard_map/psum | solution.py:12
  372.3 16.0 %fusion = f32[512,128]{1,0:T(8,128)S(1)} fusion(f32[512,128]{1,0:T(8,128)S(1)} %reshape.196, f32[512,128]{1,0:T(8,128)S(1)} %fusion.29, f32[512,4096]{0,1:T(8,128)} %all-gather.11.cloned.1.call-done, f32[128,4096]{0,1:T(8,128)} %all-reduce.2.cloned.1.call-done), kind=kOutput, calls=%fused_computation.6 | convolution fusion | flops 3221356544 | bytes 11272192 | tf_op jit(solution)/shard_map/dot_general | solution.py:91
  388.3 0.3 reshape.202
  388.7 0.2 reshape.203
  388.9 0.6 gather_fusion
  389.5 0.8 fusion.7
  (30 shorter events, 0.5 us)
Async XLA Ops:
  6.5 4.4 %copy-start = (f32[1,16,4096]{2,1,0:T(8,128)S(1)}, f32[1,16,4096]{2,1,0:T(8,128)}, u32[]{:S(2)}) copy-start(f32[1,16,4096]{2,1,0:T(8,128)} %param.11) | copy-start | bytes 786436
  6.5 48.6 %all-gather.7.cloned.1.call-start = ((), (), s32[]{:S(2)}) async-start(), calls=%async_computation.2 | async-start | bytes 2359296 | tf_op jit(solution)/shard_map/all_gather | solution.py:74
  7.7 4.2 %copy-start.2 = (s32[1,16]{1,0:T(1,128)S(1)}, s32[1,16]{1,0:T(1,128)}, u32[]{:S(2)}) copy-start(s32[1,16]{1,0:T(1,128)} %param.12) | copy-start | bytes 196
  10.9 2.9 copy-start.1
  10.9 103.3 %all-gather.5.cloned.1.call-start = ((), (), s32[]{:S(2)}) async-start(), calls=%async_computation.1 | async-start | bytes 8650752 | tf_op jit(solution)/shard_map/all_gather | solution.py:78
  11.2 3.5 copy-start.3
  13.7 240.6 %all-gather.9.cloned.1.call-start = ((), (), s32[]{:S(2)}) async-start(), calls=%async_computation.3 | async-start | bytes 2359296 | tf_op jit(solution)/shard_map/all_gather | solution.py:75
  13.8 4.0 %copy-start.4 = (s32[1,16]{1,0:T(1,128)S(1)}, s32[1,16]{1,0:T(1,128)}, u32[]{:S(2)}) copy-start(s32[1,16]{1,0:T(1,128)} %param.20) | copy-start | bytes 196
  16.6 254.0 %all-gather.11.cloned.1.call-start = ((), (), s32[]{:S(2)}) async-start(), calls=%async_computation.4 | async-start | bytes 8650752 | tf_op jit(solution)/shard_map/all_gather | solution.py:92
  134.5 116.7 %all-to-all-start = ((f32[32,512,128]{1,2,0:T(8,128)}), f32[32,512,128]{1,2,0:T(8,128)}, u32[]{:S(2)}, u32[]{:S(2)}) async-start(f32[32,512,128]{1,2,0:T(8,128)} %stack.2), calls=%async_computation | async-start | bytes 16777216 | tf_op jit(solution)/shard_map/all_to_all | solution.py:84
  140.3 232.0 %all-reduce.2.cloned.1.call-start = ((), (), s32[]{:S(2)}) async-start(), calls=%async_computation.5 | async-start | bytes 4194304 | tf_op jit(solution)/shard_map/psum | solution.py:12
Sparse Core Ops, SparseCore 0:
  11.0 44.0 all-gather.6
  57.7 56.4 all-gather.4
  116.0 40.7 all-gather.8
  159.2 111.3 all-gather.10
  272.8 99.5 all-reduce.1
